TPU v7x, 32 devices: a whole 2x2x4 slice. The times are simulated.
32 devices in a mesh: dp: 8 (over z, y), expert: 4 (over x, core).
Axes of the slice: x: 2, y: 2, z: 4, core: 2. Of those that a mesh axis runs over, the one named last changes fastest.
Arguments:
- tokens: bfloat16 [8, 1024, 2048], P('dp', 'expert'), may hold values from -6 to 6
- cotangent: bfloat16 [8, 1024, 2048], P('dp', 'expert'), may hold values from -6 to 6
- attention_routes: int32 [8, 1024, 2], P('dp'), may hold values from 0 to 3, all different within a row; in each aligned block of 256 rows (0 to 255, 256 to 511, ..., all dimensions but the last counted through in order) at most 160 rows name the same one
- feedforward_routes: int32 [8, 1024, 2], P('dp'), may hold values from 0 to 3, all different within a row; in each aligned block of 256 rows (0 to 255, 256 to 511, ..., all dimensions but the last counted through in order) at most 160 rows name the same one
- prefix_length: int32 [8], P('dp'), may hold values from 102 to 512
- gain_attention: float32 [2048], replicated, may hold values from 0.25 to 1.75
- gain_feedforward: float32 [2048], replicated, may hold values from 0.25 to 1.75
- keyvalue_weight: bfloat16 [2048, 4096], P('dp'), may hold values from -0.125 to 0.125
- router_weight: bfloat16 [2048, 8], P('dp'), may hold values from -0.25 to 0.25
- query_weight: bfloat16 [4, 2048, 2048], P('expert', 'dp'), may hold values from -0.125 to 0.125
- output_weight: bfloat16 [4, 2048, 2048], P('expert', 'dp'), may hold values from -3 to 3
- gate_weight: bfloat16 [4, 5632, 2048], P('expert', 'dp'), may hold values from -0.125 to 0.125
- up_weight: bfloat16 [4, 5632, 2048], P('expert', 'dp'), may hold values from -0.125 to 0.125
- down_weight: bfloat16 [4, 5632, 2048], P('expert', 'dp'), may hold values from -0.15625 to 0.15625
Outputs:
- layer_output: bfloat16 [8, 1024, 2048], P('dp', 'expert')
- grad_tokens: float32 [8, 1024, 2048], P('dp', 'expert')
- grad_gain_attention: float32 [2048], P('dp')
- grad_gain_feedforward: float32 [2048], P('dp')
- grad_keyvalue: float32 [2048, 4096], P('dp')
- grad_router: float32 [2048, 8], P('dp')
- grad_query: float32 [4, 2048, 2048], P('expert', 'dp')
- grad_projection: float32 [4, 2048, 2048], P('expert', 'dp')
- grad_gate: float32 [4, 5632, 2048], P('expert', 'dp')
- grad_up: float32 [4, 5632, 2048], P('expert', 'dp')
- grad_down: float32 [4, 5632, 2048], P('expert', 'dp')
Inputs may be any that keep to these rules, and one draw needn't show every extreme that they name: `attention_routes`: the two ids of a token differ. Among the 256 tokens of one device (aligned blocks of each sequence) no expert is named more than 160 times, a bound that some block reaches. `feedforward_routes`: the two ids of a token differ. Among the 256 tokens of one device (aligned blocks of each sequence) no expert is named more than 160 times, a bound that some block reaches.
All inputs are finite; a program needn't handle non-finite values.
Results may differ from a plain program's by a relative error of at most 0.025.
Values may be sent and summed in bfloat16 or wider, within the bound.
A program may use at most 448 MiB of HBM per device.

v0:
```python
import jax
import jax.numpy as jnp
from jax import lax
from jax.sharding import PartitionSpec as P

HEADS = 16
HEAD_DIM = 128
EPS = 1e-06
NEG = -1e30
HIGH = lax.Precision.HIGHEST
ACROSS = (((1,), (1,)), ((), ()))
DOWNWARD = (((0,), (0,)), ((), ()))


def norm_parts(vector, gain_vector):
    factor = lax.rsqrt(jnp.mean(vector * vector, axis=-1, keepdims=True) + EPS)
    normed = vector * factor
    return (normed * gain_vector, normed, factor)


def norm_back(incoming, gain_vector, normed, factor):
    dnormed = incoming * gain_vector
    return factor * (dnormed - normed * jnp.mean(dnormed * normed, axis=-1, keepdims=True))


def route_plan(sequence_ids, my_index, group_size, tok_rows, slot_count):
    expert_range = jnp.arange(group_size, dtype=jnp.int32)
    matches_all = (sequence_ids[:, :, None] == expert_range[None, None, :]).astype(jnp.int32)
    chosen = jnp.sum(matches_all, axis=1).reshape(group_size, tok_rows, group_size)
    ranking = jnp.cumsum(chosen, axis=1) - chosen
    slot_ids = jnp.arange(slot_count, dtype=jnp.int32)[None, :, None]
    block_pick = (expert_range == my_index).astype(jnp.int32)
    my_chosen = jnp.sum(chosen * block_pick[:, None, None], axis=0).T
    my_ranking = jnp.sum(ranking * block_pick[:, None, None], axis=0).T
    send_table = (
        my_chosen[:, None, :] * (my_ranking[:, None, :] == slot_ids).astype(jnp.int32)
    ).astype(jnp.float32)
    column_chosen = jnp.sum(chosen * block_pick[None, None, :], axis=2)
    column_ranking = jnp.sum(ranking * block_pick[None, None, :], axis=2)
    taken = column_chosen[:, None, :] * (column_ranking[:, None, :] == slot_ids).astype(jnp.int32)
    positions = (
        expert_range[:, None, None] * tok_rows
        + jnp.arange(tok_rows, dtype=jnp.int32)[None, None, :]
    )
    arrival_places = jnp.sum(taken * positions, axis=2).reshape(-1)
    my_ids = lax.dynamic_slice_in_dim(sequence_ids, my_index * tok_rows, tok_rows, 0)
    matches = (my_ids[:, :, None] == expert_range[None, None, :]).astype(jnp.float32)
    return (send_table, arrival_places, matches)


def pair_gates(logits, matches):
    selected = jnp.sum(matches * logits[:, None, :], axis=2)
    largest = jnp.max(selected, axis=1, keepdims=True)
    exponent = jnp.exp(selected - largest)
    weights = exponent / jnp.sum(exponent, axis=1, keepdims=True)
    return (weights, jnp.sum(weights[:, :, None] * matches, axis=1))


def gates_back(dgate, weights, matches):
    dweights = jnp.sum(dgate[:, None, :] * matches, axis=2)
    dselected = weights * (dweights - jnp.sum(weights * dweights, axis=1, keepdims=True))
    return jnp.sum(dselected[:, :, None] * matches, axis=1)


def merge_back(send_table, gate_table, returned):
    weighted = send_table * gate_table.T[:, None, :]
    return jnp.einsum("ect,ecd->td", weighted, returned.astype(jnp.float32), precision=HIGH)


def branch_cotangent(send_table, gate_table, returned, incoming):
    spread_grad = jnp.einsum("ect,td->ecd", send_table, incoming, precision=HIGH)
    slot_gate = jnp.sum(send_table * gate_table.T[:, None, :], axis=2)
    cotangent_rows = (spread_grad * slot_gate[:, :, None]).astype(jnp.bfloat16)
    slot_dgate = jnp.sum(spread_grad * returned.astype(jnp.float32), axis=2)
    dgate = jnp.einsum("ect,ec->te", send_table, slot_dgate, precision=HIGH)
    return (cotangent_rows, dgate)


def dispatch(rows):
    return lax.all_to_all(rows, "expert", split_axis=0, concat_axis=0, tiled=True)


def collect(rows):
    return lax.all_to_all(rows, "expert", split_axis=0, concat_axis=0, tiled=True)


def spread_rows(rows):
    return lax.all_gather(rows, "dp", axis=0, tiled=True)


def sum_rows(terms):
    return lax.psum_scatter(
        terms.astype(jnp.bfloat16), "dp", scatter_dimension=0, tiled=True
    ).astype(jnp.float32)


def send_rows(send_table, rows):
    return jnp.einsum(
        "ect,td->ecd", send_table.astype(jnp.bfloat16), rows, preferred_element_type=jnp.float32
    ).astype(jnp.bfloat16)


def per_device(
    tokens,
    cotangent,
    attention_routes,
    feedforward_routes,
    prefix_length,
    gain_attention,
    gain_feedforward,
    keyvalue_weight,
    router_weight,
    query_weight,
    output_weight,
    gate_weight,
    up_weight,
    down_weight,
):
    my_index = lax.axis_index("expert")
    group_size = lax.axis_size("expert")
    inputs = tokens[0].astype(jnp.float32)
    tok_rows = inputs.shape[0]
    model_width = inputs.shape[1]
    seq_total = tok_rows * group_size
    slot_count = 5 * 2 * tok_rows // (4 * group_size)
    query_width = HEADS * HEAD_DIM
    scaling = HEAD_DIM ** (-0.5)
    keyvalue_full, router_full, query_full, output_full = (
        lax.all_gather(keyvalue_weight, "dp", axis=0, tiled=True),
        lax.all_gather(router_weight, "dp", axis=0, tiled=True),
        lax.all_gather(query_weight[0], "dp", axis=0, tiled=True),
        lax.all_gather(output_weight[0], "dp", axis=0, tiled=True),
    )
    attention_cols = router_full[:, :group_size]
    feedforward_cols = router_full[:, group_size:]
    normed_attention, unit_attention, factor_attention = norm_parts(inputs, gain_attention)
    attention_in = normed_attention.astype(jnp.bfloat16)
    keyvalue_rows = jnp.dot(attention_in, keyvalue_full, preferred_element_type=jnp.float32).astype(
        jnp.bfloat16
    )
    keyvalue_seq = lax.all_gather(keyvalue_rows, "expert", axis=0, tiled=True)
    key_rows = keyvalue_seq[:, :query_width].reshape(seq_total, HEADS, HEAD_DIM)
    value_rows = keyvalue_seq[:, query_width:].reshape(seq_total, HEADS, HEAD_DIM)
    attend_table, attend_places, attend_matches = route_plan(
        attention_routes[0], my_index, group_size, tok_rows, slot_count
    )
    attend_logits = jnp.dot(attention_in, attention_cols, preferred_element_type=jnp.float32)
    attend_weights, attend_gate = pair_gates(attend_logits, attend_matches)
    arrived = dispatch(send_rows(attend_table, attention_in)).reshape(-1, model_width)
    queries = jnp.dot(arrived, query_full, preferred_element_type=jnp.float32).astype(jnp.bfloat16)
    queries = queries.reshape(-1, HEADS, HEAD_DIM)
    key_places = jnp.arange(seq_total, dtype=jnp.int32)
    allowed = (key_places[None, :] <= attend_places[:, None]) | (
        key_places[None, :] < prefix_length[0]
    )
    scores = (
        jnp.einsum("rhd,khd->hrk", queries, key_rows, preferred_element_type=jnp.float32) * scaling
    )
    scores = jnp.where(allowed[None], scores, NEG)
    row_max = jnp.max(scores, axis=2, keepdims=True)
    exponent = jnp.exp(scores - row_max)
    row_total = jnp.sum(exponent, axis=2, keepdims=True)
    log_total = row_max + jnp.log(row_total)
    attention_low = (exponent / row_total).astype(jnp.bfloat16)
    mixture = jnp.einsum(
        "hrk,khd->rhd", attention_low, value_rows, preferred_element_type=jnp.float32
    )
    mixture = mixture.astype(jnp.bfloat16).reshape(-1, query_width)
    attend_branch = jnp.dot(mixture, output_full, preferred_element_type=jnp.float32).astype(
        jnp.bfloat16
    )
    attend_returned = collect(attend_branch.reshape(group_size, slot_count, model_width))
    hidden = inputs + merge_back(attend_table, attend_gate, attend_returned)
    normed_feed, unit_feed, factor_feed = norm_parts(hidden, gain_feedforward)
    feed_in = normed_feed.astype(jnp.bfloat16)
    feed_table, _, feed_matches = route_plan(
        feedforward_routes[0], my_index, group_size, tok_rows, slot_count
    )
    feed_logits = jnp.dot(feed_in, feedforward_cols, preferred_element_type=jnp.float32)
    feed_weights, feed_gate = pair_gates(feed_logits, feed_matches)
    feed_rows = dispatch(send_rows(feed_table, feed_in)).reshape(-1, model_width)
    everyone = spread_rows(feed_rows)
    pre_gate = lax.dot_general(everyone, gate_weight[0], ACROSS, preferred_element_type=jnp.float32)
    pre_up = lax.dot_general(everyone, up_weight[0], ACROSS, preferred_element_type=jnp.float32)
    act_low = (pre_gate * jax.nn.sigmoid(pre_gate) * pre_up).astype(jnp.bfloat16)
    feed_branch = sum_rows(
        jnp.dot(act_low, down_weight[0], preferred_element_type=jnp.float32)
    ).astype(jnp.bfloat16)
    feed_returned = collect(feed_branch.reshape(group_size, slot_count, model_width))
    layer_output = hidden + merge_back(feed_table, feed_gate, feed_returned)
    gradient = cotangent[0].astype(jnp.float32)
    feed_cot, feed_dgate = branch_cotangent(feed_table, feed_gate, feed_returned, gradient)
    feed_dlogits = gates_back(feed_dgate, feed_weights, feed_matches)
    feed_cot_rows = dispatch(feed_cot).reshape(-1, model_width)
    cot_everyone = spread_rows(feed_cot_rows)
    sigmoid_gate = jax.nn.sigmoid(pre_gate)
    act_grad = lax.dot_general(
        cot_everyone, down_weight[0], ACROSS, preferred_element_type=jnp.float32
    )
    dgate_low = (act_grad * pre_up * sigmoid_gate * (1.0 + pre_gate * (1.0 - sigmoid_gate))).astype(
        jnp.bfloat16
    )
    dup_low = (act_grad * pre_gate * sigmoid_gate).astype(jnp.bfloat16)
    grad_gate = lax.dot_general(dgate_low, everyone, DOWNWARD, preferred_element_type=jnp.float32)
    grad_up = lax.dot_general(dup_low, everyone, DOWNWARD, preferred_element_type=jnp.float32)
    grad_down = lax.dot_general(act_low, cot_everyone, DOWNWARD, preferred_element_type=jnp.float32)
    feed_dx = sum_rows(
        jnp.dot(dgate_low, gate_weight[0], preferred_element_type=jnp.float32)
        + jnp.dot(dup_low, up_weight[0], preferred_element_type=jnp.float32)
    )
    feed_home = lax.all_to_all(
        feed_dx.reshape(group_size, slot_count, model_width).astype(jnp.bfloat16),
        "expert",
        split_axis=0,
        concat_axis=0,
        tiled=True,
    ).astype(jnp.float32)
    feed_dnorm = jnp.einsum("ect,ecd->td", feed_table, feed_home, precision=HIGH) + jnp.dot(
        feed_dlogits, feedforward_cols.astype(jnp.float32).T, precision=HIGH
    )
    grad_gain_feed = jnp.sum(feed_dnorm * unit_feed, axis=0)
    hidden_grad = gradient + norm_back(feed_dnorm, gain_feedforward, unit_feed, factor_feed)
    attend_cot, attend_dgate = branch_cotangent(
        attend_table, attend_gate, attend_returned, hidden_grad
    )
    attend_dlogits = gates_back(attend_dgate, attend_weights, attend_matches)
    attend_cot_rows = dispatch(attend_cot).reshape(-1, model_width)
    dmixture = lax.dot_general(
        attend_cot_rows, output_full, ACROSS, preferred_element_type=jnp.float32
    )
    dmixture = dmixture.astype(jnp.bfloat16).reshape(-1, HEADS, HEAD_DIM)
    grad_projection = lax.dot_general(
        mixture, attend_cot_rows, DOWNWARD, preferred_element_type=jnp.float32
    )
    scores_again = (
        jnp.einsum("rhd,khd->hrk", queries, key_rows, preferred_element_type=jnp.float32) * scaling
    )
    attention = jnp.where(allowed[None], jnp.exp(scores_again - log_total), 0.0)
    attention_again = attention.astype(jnp.bfloat16)
    dattention = jnp.einsum(
        "rhd,khd->hrk", dmixture, value_rows, preferred_element_type=jnp.float32
    )
    row_dot = jnp.sum(attention * dattention, axis=2, keepdims=True)
    dscores = (attention * (dattention - row_dot)).astype(jnp.bfloat16)
    dqueries = (
        jnp.einsum("hrk,khd->rhd", dscores, key_rows, preferred_element_type=jnp.float32) * scaling
    )
    dqueries = dqueries.astype(jnp.bfloat16).reshape(-1, query_width)
    dkeys = (
        jnp.einsum("hrk,rhd->khd", dscores, queries, preferred_element_type=jnp.float32) * scaling
    )
    dvalues = jnp.einsum(
        "hrk,rhd->khd", attention_again, dmixture, preferred_element_type=jnp.float32
    )
    grad_query = lax.dot_general(arrived, dqueries, DOWNWARD, preferred_element_type=jnp.float32)
    attend_dx = lax.dot_general(dqueries, query_full, ACROSS, preferred_element_type=jnp.float32)
    keyvalue_terms = jnp.concatenate(
        [dkeys.reshape(seq_total, query_width), dvalues.reshape(seq_total, query_width)], axis=1
    ).reshape(group_size, tok_rows, 2 * query_width)
    attend_home, keyvalue_home = (
        lax.all_to_all(
            attend_dx.reshape(group_size, slot_count, model_width).astype(jnp.bfloat16),
            "expert",
            split_axis=0,
            concat_axis=0,
            tiled=True,
        ).astype(jnp.float32),
        lax.all_to_all(
            keyvalue_terms.astype(jnp.bfloat16), "expert", split_axis=0, concat_axis=0, tiled=True
        ).astype(keyvalue_terms.dtype),
    )
    dkeyvalue = jnp.sum(keyvalue_home, axis=0).astype(jnp.bfloat16)
    attend_dnorm = (
        jnp.einsum("ect,ecd->td", attend_table, attend_home, precision=HIGH)
        + lax.dot_general(dkeyvalue, keyvalue_full, ACROSS, preferred_element_type=jnp.float32)
        + jnp.dot(attend_dlogits, attention_cols.astype(jnp.float32).T, precision=HIGH)
    )
    grad_keyvalue = lax.dot_general(
        attention_in, dkeyvalue, DOWNWARD, preferred_element_type=jnp.float32
    )
    grad_router = jnp.concatenate(
        [
            jnp.dot(attention_in.astype(jnp.float32).T, attend_dlogits, precision=HIGH),
            jnp.dot(feed_in.astype(jnp.float32).T, feed_dlogits, precision=HIGH),
        ],
        axis=1,
    )
    grad_gain_attend = jnp.sum(attend_dnorm * unit_attention, axis=0)
    grad_tokens = hidden_grad + norm_back(
        attend_dnorm, gain_attention, unit_attention, factor_attention
    )
    reduced = (
        lax.psum_scatter(
            grad_keyvalue.astype(jnp.bfloat16), "dp", scatter_dimension=0, tiled=True
        ).astype(jnp.float32),
        lax.psum_scatter(
            grad_router.astype(jnp.bfloat16), "dp", scatter_dimension=0, tiled=True
        ).astype(jnp.float32),
        lax.psum_scatter(
            grad_query.astype(jnp.bfloat16), "dp", scatter_dimension=0, tiled=True
        ).astype(jnp.float32),
        lax.psum_scatter(
            grad_projection.astype(jnp.bfloat16), "dp", scatter_dimension=0, tiled=True
        ).astype(jnp.float32),
        lax.psum_scatter(
            grad_gain_attend.astype(jnp.bfloat16), "dp", scatter_dimension=0, tiled=True
        ).astype(jnp.float32),
        lax.psum_scatter(
            grad_gain_feed.astype(jnp.bfloat16), "dp", scatter_dimension=0, tiled=True
        ).astype(jnp.float32),
    )
    shared = (
        lax.psum(reduced[0].astype(jnp.bfloat16), "expert").astype(jnp.float32),
        lax.psum(reduced[1].astype(jnp.bfloat16), "expert").astype(jnp.float32),
        lax.psum(reduced[4].astype(jnp.bfloat16), "expert").astype(jnp.float32),
        lax.psum(reduced[5].astype(jnp.bfloat16), "expert").astype(jnp.float32),
    )
    return (
        layer_output.astype(jnp.bfloat16)[None],
        grad_tokens[None],
        shared[2],
        shared[3],
        shared[0],
        shared[1],
        reduced[2][None],
        reduced[3][None],
        grad_gate[None],
        grad_up[None],
        grad_down[None],
    )


def solution(mesh):
    in_specs = (
        P("dp", "expert", None),
        P("dp", "expert", None),
        P("dp", None, None),
        P("dp", None, None),
        P("dp"),
        P(),
        P(),
        P("dp", None),
        P("dp", None),
        P("expert", "dp", None),
        P("expert", "dp", None),
        P("expert", "dp", None),
        P("expert", "dp", None),
        P("expert", "dp", None),
    )
    out_specs = (
        P("dp", "expert", None),
        P("dp", "expert", None),
        P("dp"),
        P("dp"),
        P("dp", None),
        P("dp", None),
        P("expert", "dp", None),
        P("expert", "dp", None),
        P("expert", "dp", None),
        P("expert", "dp", None),
        P("expert", "dp", None),
    )
    return jax.shard_map(
        per_device, mesh=mesh, in_specs=in_specs, out_specs=out_specs, check_vma=False
    )
```

profile of v0, /device:TPU:0, one launch (start us, length us, event | category | flops | bytes accessed | tf_op | source)
XLA Modules:
  0.0 3382.4 jit_solution(1048255030446471202)
XLA Ops:
  10.3 230.2 %all-gather.9.cloned.1.call-done = bf16[2048,4096]{1,0:T(8,128)(2,1)} async-done(((bf16[256,4096]{1,0:T(8,128)(2,1)}), bf16[2048,4096]{1,0:T(8,128)(2,1)}) %all-gather.9.cloned.1.call-update) | async-done | bytes 16777232 | tf_op jit(solution)/shard_map/all_gather | solution.py:129
  240.5 12.0 convolution_convert_fusion.4
  275.2 27.9 all-to-all-done
  303.1 62.6 %all-gather.17.cloned.1.call-done = bf16[1,2048,2048]{2,1,0:T(8,128)(2,1)} async-done(((bf16[1,256,2048]{2,1,0:T(8,128)(2,1)}), bf16[1,2048,2048]{2,1,0:T(8,128)(2,1)}) %all-gather.17.cloned.1.call-update) | async-done | bytes 8388624 | tf_op jit(solution)/shard_map/all_gather | solution.py:131
  365.7 10.6 fusion.20
  381.0 43.4 %all-gather.11.cloned.1.call-done = bf16[1024,4096]{1,0:T(8,128)(2,1)} async-done(((bf16[256,4096]{1,0:T(8,128)(2,1)}), bf16[1024,4096]{1,0:T(8,128)(2,1)}) %all-gather.11.cloned.1.call-update) | async-done | bytes 8388624 | tf_op jit(solution)/shard_map/all_gather | solution.py:141
  437.0 20.9 select_reduce_fusion
  457.9 18.9 fusion
  477.4 20.9 fusion.62
  498.4 53.0 %all-gather.19.cloned.1.call-done = bf16[1,2048,2048]{2,1,0:T(8,128)(2,1)} async-done(((bf16[1,256,2048]{2,1,0:T(8,128)(2,1)}), bf16[1,2048,2048]{2,1,0:T(8,128)(2,1)}) %all-gather.19.cloned.1.call-update) | async-done | bytes 8388624 | tf_op jit(solution)/shard_map/all_gather | solution.py:132
  551.3 9.9 fusion.29
  566.1 30.4 all_gather.21
  606.4 34.6 %all_to_all.45 = bf16[4,160,2048]{2,1,0:T(8,128)(2,1)} all-to-all(bf16[4,160,2048]{2,1,0:T(8,128)(2,1)S(1)} %convolution_convert_fusion.5), channel_id=1, replica_groups=mesh['dp'=8,'expert'=4] {'expert'}, dimensions={0} | all-to-all | bytes 5242880 | tf_op jit(solution)/shard_map/all_to_all | solution.py:80
  641.1 399.0 %all-gather.13.cloned.1.call-done = bf16[5120,2048]{1,0:T(8,128)(2,1)} async-done(((bf16[640,2048]{1,0:T(8,128)(2,1)}), bf16[5120,2048]{1,0:T(8,128)(2,1)}) %all-gather.13.cloned.1.call-update) | async-done | bytes 20971536 | tf_op jit(solution)/shard_map/all_gather | solution.py:88
  1040.1 22.4 fusion.44
  1062.5 29.8 multiply_convert_fusion.3
  1092.3 23.3 convolution_convert_fusion
  1115.6 343.6 %reduce-scatter.7.cloned.1.call-done = bf16[640,2048]{1,0:T(8,128)(2,1)} async-done(((bf16[5120,2048]{1,0:T(8,128)(2,1)}), bf16[640,2048]{1,0:T(8,128)(2,1)}) %reduce-scatter.7.cloned.1.call-update) | async-done | bytes 2621456 | tf_op jit(solution)/shard_map/reduce_scatter | solution.py:92
  1466.1 29.0 all-to-all-done.3
  1505.8 34.6 %all_to_all.46 = bf16[4,160,2048]{2,1,0:T(8,128)(2,1)} all-to-all(bf16[4,160,2048]{2,1,0:T(8,128)(2,1)S(1)} %multiply_convert_fusion.7), channel_id=1, replica_groups=mesh['dp'=8,'expert'=4] {'expert'}, dimensions={0} | all-to-all | bytes 5242880 | tf_op jit(solution)/shard_map/all_to_all | solution.py:80
  1540.4 400.1 %all-gather.15.cloned.1.call-done = bf16[5120,2048]{1,0:T(8,128)(2,1)} async-done(((bf16[640,2048]{1,0:T(8,128)(2,1)}), bf16[5120,2048]{1,0:T(8,128)(2,1)}) %all-gather.15.cloned.1.call-update) | async-done | bytes 20971536 | tf_op jit(solution)/shard_map/all_gather | solution.py:88
  1940.6 42.0 %multiply_convert_fusion.1 = (bf16[5120,704]{0,1:T(8,128)(2,1)}, bf16[5120,704]{0,1:T(8,128)(2,1)}) fusion(f32[5120,704]{0,1:T(8,128)} %fusion.44, f32[5120,704]{0,1:T(8,128)} %get-tuple-element.45, bf16[5120,2048]{1,0:T(8,128)(2,1)} %all-gather.15.cloned.1.call-done, bf16[1,704,2048]{2,1,0:T(8,128)(2,1)S(1)} %copy-done), kind=kOutput, calls=%fused_computation.14 | convolution fusion | flops 14810808320 | bytes 67108864 | tf_op jit(solution)/shard_map/dot_general | solution.py:197
  1982.6 27.1 fusion.42
  2009.7 28.7 add_convert_fusion
  2038.4 343.6 %reduce-scatter.9.cloned.1.call-done = bf16[640,2048]{1,0:T(8,128)(2,1)} async-done(((bf16[5120,2048]{1,0:T(8,128)(2,1)}), bf16[640,2048]{1,0:T(8,128)(2,1)}) %reduce-scatter.9.cloned.1.call-update) | async-done | bytes 2621456 | tf_op jit(solution)/shard_map/reduce_scatter | solution.py:92
  2387.1 31.1 all-to-all-done.5
  2438.2 31.2 all-to-all-done.6
  2470.9 10.3 fusion.23
  2484.4 18.0 convert_bitcast_fusion
  2502.5 35.8 %multiply_reduce_fusion = (f32[16,640]{1,0:T(8,128)S(1)}, f32[16,640,1024]{2,1,0:T(8,128)}) fusion(f32[16,640,1024]{2,1,0:T(8,128)} %get-tuple-element.41, f32[16,640]{1,0:T(8,128)S(1)} %log_add_fusion, pred[640,1024]{1,0:T(8,128)(4,1)S(1)} %copy-done.7, bf16[640,16,128]{0,2,1:T(8,128)(2,1)S(1)} %bitcast.245, bf16[128,16,8,128]{3,2,1,0:T(8,128)(2,1)} %get-tuple-element.36), kind=kOutput, calls=%fused_computation.1 | convolution fusion | flops 2736773120 | bytes 91439104 | tf_op jit(solution)/shard_map/rhd,khd->hrk/dot_general | solution.py:240
  2550.8 34.3 %multiply_convert_fusion = bf16[16,640,1024]{2,1,0:T(8,128)(2,1)} fusion(f32[16,640,1024]{2,1,0:T(8,128)} %get-tuple-element.50, f32[16,640,1024]{2,1,0:T(8,128)} %get-tuple-element.41, f32[16,640]{1,0:T(8,128)S(1)} %get-tuple-element.49, f32[16,640]{1,0:T(8,128)S(1)} %log_add_fusion, pred[640,1024]{1,0:T(8,128)(4,1)S(1)} %copy-done.7), kind=kLoop, calls=%fused_computation | loop fusion | flops 62914560 | bytes 105594880 | tf_op jit(solution)/shard_map/convert_element_type | solution.py:244
  2585.1 12.5 fusion.14
  2625.9 90.6 %all-to-all-done.8 = bf16[4,256,4096]{1,2,0:T(8,128)(2,1)} async-done(((bf16[4,256,4096]{1,2,0:T(8,128)(2,1)}), bf16[4,256,4096]{1,2,0:T(8,128)(2,1)}, u32[]{:S(2)}, u32[]{:S(2)}) %all-to-all-start.8) | async-done | bytes 8388640 | tf_op jit(solution)/shard_map/all_to_all | solution.py:268
  2722.9 9.9 convolution_convert_fusion.1
  2734.6 10.9 convolution_convert_fusion.2
  2747.5 11.7 multiply_convert_fusion.5
  2759.2 11.7 convolution_convert_fusion.3
  2778.3 21.5 convolution_bitcast_fusion
  2799.8 17.3 convolution_bitcast_fusion.1
  2827.1 10.8 fusion.26
  2842.5 21.7 convolution_bitcast_fusion.2
  2864.3 9.6 all-to-all-done.7
  2879.7 12.9 convolution_add_fusion.2
  2897.4 20.1 all-reduce.2
  2931.0 84.0 %reduce-scatter.11.cloned.1.call-done = bf16[256,4096]{1,0:T(8,128)(2,1)} async-done(((bf16[2048,4096]{1,0:T(8,128)(2,1)}), bf16[256,4096]{1,0:T(8,128)(2,1)}) %reduce-scatter.11.cloned.1.call-update) | async-done | bytes 2097168 | tf_op jit(solution)/shard_map/reduce_scatter | solution.py:293
  3015.0 152.1 %reduce-scatter.17.cloned.1.call-done = bf16[256,2048]{1,0:T(8,128)(2,1)} async-done(((bf16[2048,2048]{1,0:T(8,128)(2,1)}), bf16[256,2048]{1,0:T(8,128)(2,1)}) %reduce-scatter.17.cloned.1.call-update) | async-done | bytes 1048592 | tf_op jit(solution)/shard_map/reduce_scatter | solution.py:302
  3170.1 148.6 %reduce-scatter.15.cloned.1.call-done = bf16[256,2048]{1,0:T(8,128)(2,1)} async-done(((bf16[2048,2048]{1,0:T(8,128)(2,1)}), bf16[256,2048]{1,0:T(8,128)(2,1)}) %reduce-scatter.15.cloned.1.call-update) | async-done | bytes 1048592 | tf_op jit(solution)/shard_map/reduce_scatter | solution.py:299
  3321.5 50.1 %all-reduce.6.cloned.1.call-done = bf16[256,4096]{1,0:T(8,128)(2,1)} async-done(((bf16[256,4096]{1,0:T(8,128)(2,1)}), bf16[256,4096]{1,0:T(8,128)(2,1)}) %all-reduce.6.cloned.1.call-update) | async-done | bytes 2097168 | tf_op jit(solution)/shard_map/psum | solution.py:313
  (290 shorter events, 210.6 us)
Async XLA Ops:
  7.2 1085.2 %copy-start = (bf16[1,704,2048]{2,1,0:T(8,128)(2,1)S(1)}, bf16[1,704,2048]{2,1,0:T(8,128)(2,1)}, u32[]{:S(2)}) copy-start(bf16[1,704,2048]{2,1,0:T(8,128)(2,1)} %param.27) | copy-start | bytes 8650756
  7.2 233.3 %copy-start.27 = (f32[2048]{0:T(1024)S(1)}, f32[2048]{0:T(1024)}, u32[]{:S(2)}) copy-start(f32[2048]{0:T(1024)} %param.19) | copy-start | bytes 24580
  7.2 233.3 %all-gather.9.cloned.1.call-start = ((), (), s32[]{:S(2)}) async-start(), calls=%async_computation.15 | async-start | bytes 18874368 | tf_op jit(solution)/shard_map/all_gather | solution.py:129
  7.9 357.8 %all-gather.17.cloned.1.call-start = ((), (), s32[]{:S(2)}) async-start(), calls=%async_computation.26 | async-start | bytes 9437184 | tf_op jit(solution)/shard_map/all_gather | solution.py:131
  8.7 415.7 %all-gather.11.cloned.1.call-start = ((), (), s32[]{:S(2)}) async-start(), calls=%async_computation.16 | async-start | bytes 10485760 | tf_op jit(solution)/shard_map/all_gather | solution.py:141
  10.3 253.2 %copy-start.47 = (f32[256]{0:T(256)}, f32[256]{0:T(256)S(1)}, u32[]{:S(2)}) copy-start(f32[256]{0:T(256)S(1)} %add_rsqrt_fusion.1) | copy-start | bytes 3076
  10.3 242.3 %copy-start.64 = (s32[1,1024,2]{1,2,0:T(2,128)S(1)}, s32[1,1024,2]{1,2,0:T(2,128)}, u32[]{:S(2)}) copy-start(s32[1,1024,2]{1,2,0:T(2,128)} %param.17) | copy-start | bytes 24580
  10.3 247.6 %copy-start.63 = (s32[1,1024,2]{1,2,0:T(2,128)S(1)}, s32[1,1024,2]{1,2,0:T(2,128)}, u32[]{:S(2)}) copy-start(s32[1,1024,2]{1,2,0:T(2,128)} %param.16) | copy-start | bytes 24580
  263.4 2154.8 %copy-start.23 = (s32[256,4]{0,1:T(4,128)}, s32[256,4]{0,1:T(4,128)S(1)}, u32[]{:S(2)}) copy-start(s32[256,4]{0,1:T(4,128)S(1)} %get-tuple-element.17) | copy-start | bytes 12292
  263.4 2154.8 %copy-start.25 = (s32[256,4]{0,1:T(4,128)}, s32[256,4]{0,1:T(4,128)S(1)}, u32[]{:S(2)}) copy-start(s32[256,4]{0,1:T(4,128)S(1)} %get-tuple-element.18) | copy-start | bytes 12292
  267.2 35.9 %all-to-all-start = ((bf16[4,160,2048]{2,1,0:T(8,128)(2,1)}), bf16[4,160,2048]{2,1,0:T(8,128)(2,1)}, u32[]{:S(2)}, u32[]{:S(2)}) async-start(bf16[4,160,2048]{2,1,0:T(8,128)(2,1)} %convolution_convert_fusion.6), calls=%async_computation | async-start | bytes 5242880 | tf_op jit(solution)/shard_map/all_to_all | solution.py:80
  271.7 279.6 %all-gather.19.cloned.1.call-start = ((), (), s32[]{:S(2)}) async-start(), calls=%async_computation.27 | async-start | bytes 9437184 | tf_op jit(solution)/shard_map/all_gather | solution.py:132
  275.2 201.6 %copy-start.6 = (pred[640,1024]{1,0:T(8,128)(4,1)}, pred[640,1024]{1,0:T(8,128)(4,1)S(1)}, u32[]{:S(2)}) copy-start(pred[640,1024]{1,0:T(8,128)(4,1)S(1)} %fusion.48) | copy-start | bytes 1966084
  561.3 35.9 %copy-start.48 = (f32[256]{0:T(256)S(1)}, f32[256]{0:T(256)}, u32[]{:S(2)}) copy-start(f32[256]{0:T(256)} %copy-done.47) | copy-start | bytes 3076
  561.3 37.8 %copy-start.38 = (s32[256,4]{0,1:T(4,128)S(1)}, s32[256,4]{0,1:T(4,128)}, u32[]{:S(2)}) copy-start(s32[256,4]{0,1:T(4,128)} %copy-done.37) | copy-start | bytes 12292
  561.3 37.8 %copy-start.42 = (s32[256,4]{0,1:T(4,128)S(1)}, s32[256,4]{0,1:T(4,128)}, u32[]{:S(2)}) copy-start(s32[256,4]{0,1:T(4,128)} %copy-done.41) | copy-start | bytes 12292
  561.3 37.8 %all-to-all-start.1 = ((bf16[4,160,2048]{2,1,0:T(8,128)(2,1)}), bf16[4,160,2048]{2,1,0:T(8,128)(2,1)}, u32[]{:S(2)}, u32[]{:S(2)}) async-start(bf16[4,160,2048]{2,1,0:T(8,128)(2,1)} %bitcast.250), calls=%async_computation.1 | async-start | bytes 5242880 | tf_op jit(solution)/shard_map/all_to_all | solution.py:84
  566.0 39.2 %copy-start.30 = (f32[2048]{0:T(1024)S(1)}, f32[2048]{0:T(1024)}, u32[]{:S(2)}) copy-start(f32[2048]{0:T(1024)} %param.20) | copy-start | bytes 24580
  566.0 474.0 %all-gather.13.cloned.1.call-start = ((), (), s32[]{:S(2)}) async-start(), calls=%async_computation.17 | async-start | bytes 23592960 | tf_op jit(solution)/shard_map/all_gather | solution.py:88
  596.5 1826.1 %copy-start.17 = (bf16[2048,8]{0,1:T(8,128)(2,1)}, bf16[2048,8]{0,1:T(8,128)(2,1)S(1)}, u32[]{:S(2)}) copy-start(bf16[2048,8]{0,1:T(8,128)(2,1)S(1)} %all_gather.21) | copy-start | bytes 98308
  603.9 37.1 %copy-start.53 = (f32[256]{0:T(256)}, f32[256]{0:T(256)S(1)}, u32[]{:S(2)}) copy-start(f32[256]{0:T(256)S(1)} %add_rsqrt_fusion) | copy-start | bytes 3076
  605.5 35.5 %copy-start.10 = (bf16[256,2048]{1,0:T(8,128)(2,1)}, bf16[256,2048]{1,0:T(8,128)(2,1)S(1)}, u32[]{:S(2)}) copy-start(bf16[256,2048]{1,0:T(8,128)(2,1)S(1)} %multiply_convert_fusion.8) | copy-start | bytes 3145732
  641.0 818.1 %reduce-scatter.7.cloned.1.call-start = ((), (), s32[]{:S(2)}) async-start(), calls=%async_computation.18 | async-start | bytes 23592960 | tf_op jit(solution)/shard_map/reduce_scatter | solution.py:92
  1459.2 36.0 %all-to-all-start.3 = ((bf16[4,160,2048]{2,1,0:T(8,128)(2,1)}), bf16[4,160,2048]{2,1,0:T(8,128)(2,1)}, u32[]{:S(2)}, u32[]{:S(2)}) async-start(bf16[4,160,2048]{2,1,0:T(8,128)(2,1)} %bitcast.251), calls=%async_computation.4 | async-start | bytes 5242880 | tf_op jit(solution)/shard_map/all_to_all | solution.py:84
  1463.8 476.8 %all-gather.15.cloned.1.call-start = ((), (), s32[]{:S(2)}) async-start(), calls=%async_computation.19 | async-start | bytes 23592960 | tf_op jit(solution)/shard_map/all_gather | solution.py:88
  1502.7 37.7 %copy-start.45 = (f32[256,4]{0,1:T(4,128)}, f32[256,4]{0,1:T(4,128)S(1)}, u32[]{:S(2)}) copy-start(f32[256,4]{0,1:T(4,128)S(1)} %get-tuple-element.21) | copy-start | bytes 12292
  1540.4 841.5 %reduce-scatter.9.cloned.1.call-start = ((), (), s32[]{:S(2)}) async-start(), calls=%async_computation.20 | async-start | bytes 23592960 | tf_op jit(solution)/shard_map/reduce_scatter | solution.py:92
  2038.3 348.5 %copy-start.39 = (s32[256,4]{0,1:T(4,128)S(1)}, s32[256,4]{0,1:T(4,128)}, u32[]{:S(2)}) copy-start(s32[256,4]{0,1:T(4,128)} %copy-done.37) | copy-start | bytes 12292
  2038.3 348.5 %copy-start.43 = (s32[256,4]{0,1:T(4,128)S(1)}, s32[256,4]{0,1:T(4,128)}, u32[]{:S(2)}) copy-start(s32[256,4]{0,1:T(4,128)} %copy-done.41) | copy-start | bytes 12292
  2038.4 348.5 %copy-start.61 = (f32[256,4]{0,1:T(4,128)S(1)}, f32[256,4]{0,1:T(4,128)}, u32[]{:S(2)}) copy-start(f32[256,4]{0,1:T(4,128)} %copy-done.60) | copy-start | bytes 12292
  2381.9 40.7 %copy-start.4 = (f32[256,2048]{1,0:T(8,128)S(1)}, f32[256,2048]{1,0:T(8,128)}, u32[]{:S(2)}) copy-start(f32[256,2048]{1,0:T(8,128)} %copy-done.3) | copy-start | bytes 6291460
  2381.9 40.7 %copy-start.31 = (f32[2048]{0:T(1024)S(1)}, f32[2048]{0:T(1024)}, u32[]{:S(2)}) copy-start(f32[2048]{0:T(1024)} %param.20) | copy-start | bytes 24580
  2381.9 40.7 %copy-start.54 = (f32[256]{0:T(256)S(1)}, f32[256]{0:T(256)}, u32[]{:S(2)}) copy-start(f32[256]{0:T(256)} %copy-done.53) | copy-start | bytes 3076
  2381.9 36.3 %all-to-all-start.5 = ((bf16[4,160,2048]{2,1,0:T(8,128)(2,1)}), bf16[4,160,2048]{2,1,0:T(8,128)(2,1)}, u32[]{:S(2)}, u32[]{:S(2)}) async-start(bf16[4,160,2048]{2,1,0:T(8,128)(2,1)} %bitcast.252), calls=%async_computation.7 | async-start | bytes 5242880 | tf_op jit(solution)/shard_map/all_to_all | solution.py:211
  2434.0 35.5 %all-to-all-start.6 = ((bf16[4,160,2048]{2,1,0:T(8,128)(2,1)}), bf16[4,160,2048]{2,1,0:T(8,128)(2,1)S(1)}, u32[]{:S(2)}, u32[]{:S(2)}) async-start(bf16[4,160,2048]{2,1,0:T(8,128)(2,1)} %get-tuple-element.39), calls=%async_computation.8 | async-start | bytes 5242880 | tf_op jit(solution)/shard_map/all_to_all | solution.py:80
  2550.8 34.3 %copy-start.2 = (bf16[640,2048]{0,1:T(8,128)(2,1)S(1)}, bf16[640,2048]{0,1:T(8,128)(2,1)}, u32[]{:S(2)}) copy-start(bf16[640,2048]{0,1:T(8,128)(2,1)} %copy.103) | copy-start | bytes 7864324
  2617.5 99.0 %all-to-all-start.8 = ((bf16[4,256,4096]{1,2,0:T(8,128)(2,1)}), bf16[4,256,4096]{1,2,0:T(8,128)(2,1)}, u32[]{:S(2)}, u32[]{:S(2)}) async-start(bf16[4,256,4096]{1,2,0:T(8,128)(2,1)} %pad_maximum_fusion), calls=%async_computation.10 | async-start | bytes 16777216 | tf_op jit(solution)/shard_map/all_to_all | solution.py:268
  2623.3 294.5 %reduce-scatter.13.cloned.1.call-start = ((), (), s32[]{:S(2)}) async-start(), calls=%async_computation.23 | async-start | bytes 36864 | tf_op jit(solution)/shard_map/reduce_scatter | solution.py:296
  2624.5 98.5 %copy-start.56 = (f32[256,4]{0,1:T(4,128)}, f32[256,4]{0,1:T(4,128)S(1)}, u32[]{:S(2)}) copy-start(f32[256,4]{0,1:T(4,128)S(1)} %select_reduce_fusion.1) | copy-start | bytes 12292
  2625.8 389.2 %reduce-scatter.11.cloned.1.call-start = ((), (), s32[]{:S(2)}) async-start(), calls=%async_computation.21 | async-start | bytes 18874368 | tf_op jit(solution)/shard_map/reduce_scatter | solution.py:293
  2732.9 434.2 %reduce-scatter.17.cloned.1.call-start = ((), (), s32[]{:S(2)}) async-start(), calls=%async_computation.25 | async-start | bytes 9437184 | tf_op jit(solution)/shard_map/reduce_scatter | solution.py:302
  2745.6 573.1 %reduce-scatter.15.cloned.1.call-start = ((), (), s32[]{:S(2)}) async-start(), calls=%async_computation.24 | async-start | bytes 9437184 | tf_op jit(solution)/shard_map/reduce_scatter | solution.py:299
  2837.9 35.9 %all-to-all-start.7 = ((bf16[4,160,2048]{2,1,0:T(8,128)(2,1)}), bf16[4,160,2048]{2,1,0:T(8,128)(2,1)}, u32[]{:S(2)}, u32[]{:S(2)}) async-start(bf16[4,160,2048]{2,1,0:T(8,128)(2,1)} %fusion.26), calls=%async_computation.9 | async-start | bytes 5242880 | tf_op jit(solution)/shard_map/all_to_all | solution.py:261
  2842.5 529.1 %all-reduce.6.cloned.1.call-start = ((), (), s32[]{:S(2)}) async-start(), calls=%async_computation.22 | async-start | bytes 4194304 | tf_op jit(solution)/shard_map/psum | solution.py:313
  2892.7 33.1 copy-start.32
  2892.7 33.1 copy-start.55
  2892.7 33.1 copy-start.66
  3167.1 208.5 %copy-start.1 = (bf16[1,704,2048]{2,1,0:T(8,128)(2,1)S(1)}, bf16[1,704,2048]{2,1,0:T(8,128)(2,1)}, u32[]{:S(2)}) copy-start(bf16[1,704,2048]{2,1,0:T(8,128)(2,1)} %param.27) | copy-start | bytes 8650756
  (49 other events, 505.6 us)
Sparse Core Ops, SparseCore 0:
  10.2 230.2 all-gather.8
  242.6 123.0 all-gather.16
  367.9 56.4 all-gather.10
  426.4 124.9 all-gather.18
  641.2 398.8 all-gather.12
  1115.8 343.3 reduce-scatter.6
  1540.5 400.0 all-gather.14
  2038.5 343.4 reduce-scatter.8
  2627.2 53.1 reduce-scatter.12
  2733.0 281.9 reduce-scatter.10
  3019.1 148.0 reduce-scatter.16
  3170.6 148.0 reduce-scatter.14
  3321.2 50.3 all-reduce.5
where the time goes:
time: 3390 us; the launch traced here: 3380 us
  waiting for transfers between devices  2530 us (75%)
  matrix products  506 us (15%)
  blocking collectives  126 us (4%)
  other arithmetic  101 us (3%)
  local copies, waits for them, and re-layouts  66.8 us (2%)
  starting transfers between devices  34.3 us (1%)
    all_gather x2, waiting for transfers between devices, spread_rows(): return lax.all_gather(rows, 'dp', axis=0, tiled=True)  799 us
    reduce_scatter x2, waiting for transfers between devices, sum_rows(): lax.psum_scatter(terms.astype(jnp.bfloat16), 'dp', scatter_dimension=0, t...  687 us
    all_gather x1, waiting for transfers between devices, per_device(): lax.all_gather(keyvalue_weight, 'dp', axis=0, tiled=True)  230 us
    reduce_scatter x1, waiting for transfers between devices, per_device(): lax.psum_scatter(grad_projection.astype(jnp.bfloat16), 'dp', scatter_dime...  152 us
    reduce_scatter x1, waiting for transfers between devices, per_device(): lax.psum_scatter(grad_query.astype(jnp.bfloat16), 'dp', scatter_dimension...  149 us
    all_to_all x1, waiting for transfers between devices, per_device(): lax.all_to_all(keyvalue_terms.astype(jnp.bfloat16), 'expert', split_axis=...  90.6 us
    reduce_scatter x1, waiting for transfers between devices, per_device(): lax.psum_scatter(grad_keyvalue.astype(jnp.bfloat16), 'dp', scatter_dimens...  84 us
    all_to_all x2, blocking collectives, dispatch(): lax.all_to_all(rows, 'expert', split_axis=0, concat_axis=0, tiled=True)  69.2 us
  transfers between devices with their start and end apart: 20, of which 18 were waited for; matrix products, arithmetic and copies ran while one was open for 9% of the time, Pallas kernels for 0%

commit v1 on v0

--- a/solution.py
+++ b/solution.py
@@ -10,6 +10,18 @@
 HIGH = lax.Precision.HIGHEST
 ACROSS = (((1,), (1,)), ((), ()))
 DOWNWARD = (((0,), (0,)), ((), ()))
+
+
+def collect_2(shard, axis, dim):
+    ways, here = (lax.axis_size(axis), lax.axis_index(axis))
+    grown, reach = (shard, 1)
+    while reach < ways:
+        theirs = lax.ppermute(grown, axis, [(d, d ^ reach) for d in range(ways)])
+        mine_first = jnp.concatenate([grown, theirs], axis=dim)
+        theirs_first = jnp.concatenate([theirs, grown], axis=dim)
+        grown = jnp.where(here & reach == 0, mine_first, theirs_first)
+        reach = 2 * reach
+    return grown
 
 
 def norm_parts(vector, gain_vector):
@@ -85,7 +97,7 @@
 
 
 def spread_rows(rows):
-    return lax.all_gather(rows, "dp", axis=0, tiled=True)
+    return collect_2(rows, "dp", 0)
 
 
 def sum_rows(terms):

time: 3390 us -> 3890 us (1.15)
  waiting for transfers between devices: 2530 us -> 2970 us
  other arithmetic: 101 us -> 148 us
    ppermute x0 -> x6, waiting for transfers between devices: none -> 1240 us  [collect_2(): theirs = lax.ppermute(grown, axis, [(d, d ^ reach) for d in range(ways)])]
    all_gather x2 -> x0, waiting for transfers between devices: 799 us -> none  [spread_rows(): return lax.all_gather(rows, 'dp', axis=0, tiled=True)]
    select_n x0 -> x4, other arithmetic: none -> 46.3 us  [collect_2(): grown = jnp.where(here & reach == 0, mine_first, theirs_first)]
  transfers between devices with their start and end apart: 20 -> 24, of which waited for: 18 -> 22; matrix products, arithmetic and copies ran while one was open for 9% -> 8% of each run, Pallas kernels for 0% -> 0%
where the time goes in v1:
time: 3890 us; the launch traced here: 3880 us
  waiting for transfers between devices  2970 us (76%)
  matrix products  519 us (13%)
  other arithmetic  148 us (4%)
  blocking collectives  126 us (3%)
  local copies, waits for them, and re-layouts  71.4 us (2%)
    ppermute x6, waiting for transfers between devices, collect_2(): theirs = lax.ppermute(grown, axis, [(d, d ^ reach) for d in range(ways)])  1240 us
    reduce_scatter x2, waiting for transfers between devices, sum_rows(): lax.psum_scatter(terms.astype(jnp.bfloat16), 'dp', scatter_dimension=0, t...  685 us
    all_gather x1, waiting for transfers between devices, per_device(): lax.all_gather(keyvalue_weight, 'dp', axis=0, tiled=True)  230 us
    reduce_scatter x1, waiting for transfers between devices, per_device(): lax.psum_scatter(grad_projection.astype(jnp.bfloat16), 'dp', scatter_dime...  152 us
    reduce_scatter x1, waiting for transfers between devices, per_device(): lax.psum_scatter(grad_query.astype(jnp.bfloat16), 'dp', scatter_dimension...  149 us
    all_to_all x1, waiting for transfers between devices, per_device(): lax.all_to_all(keyvalue_terms.astype(jnp.bfloat16), 'expert', split_axis=...  90.5 us
    reduce_scatter x1, waiting for transfers between devices, per_device(): lax.psum_scatter(grad_keyvalue.astype(jnp.bfloat16), 'dp', scatter_dimens...  82 us
  transfers between devices with their start and end apart: 24, of which 22 were waited for; matrix products, arithmetic and copies ran while one was open for 8% of the time, Pallas kernels for 0%

profile of v1, /device:TPU:0, one launch (start us, length us, event | category | flops | bytes accessed | tf_op | source)
XLA Modules:
  0.0 3884.0 jit_solution(10468117140742765973)
XLA Ops:
  10.3 230.2 %all-gather.7.cloned.1.call-done = bf16[2048,4096]{1,0:T(8,128)(2,1)} async-done(((bf16[256,4096]{1,0:T(8,128)(2,1)}), bf16[2048,4096]{1,0:T(8,128)(2,1)}) %all-gather.7.cloned.1.call-update) | async-done | bytes 16777232 | tf_op jit(solution)/shard_map/all_gather | solution.py:141
  240.5 12.0 convolution_convert_fusion.4
  275.3 27.9 all-to-all-done
  303.1 62.7 %all-gather.11.cloned.1.call-done = bf16[1,2048,2048]{2,1,0:T(8,128)(2,1)} async-done(((bf16[1,256,2048]{2,1,0:T(8,128)(2,1)}), bf16[1,2048,2048]{2,1,0:T(8,128)(2,1)}) %all-gather.11.cloned.1.call-update) | async-done | bytes 8388624 | tf_op jit(solution)/shard_map/all_gather | solution.py:143
  381.0 43.4 %all-gather.9.cloned.1.call-done = bf16[1024,4096]{1,0:T(8,128)(2,1)} async-done(((bf16[256,4096]{1,0:T(8,128)(2,1)}), bf16[1024,4096]{1,0:T(8,128)(2,1)}) %all-gather.9.cloned.1.call-update) | async-done | bytes 8388624 | tf_op jit(solution)/shard_map/all_gather | solution.py:153
  437.0 20.9 select_reduce_fusion
  458.0 18.9 fusion
  477.5 20.9 fusion.62
  498.4 53.0 %all-gather.13.cloned.1.call-done = bf16[1,2048,2048]{2,1,0:T(8,128)(2,1)} async-done(((bf16[1,256,2048]{2,1,0:T(8,128)(2,1)}), bf16[1,2048,2048]{2,1,0:T(8,128)(2,1)}) %all-gather.13.cloned.1.call-update) | async-done | bytes 8388624 | tf_op jit(solution)/shard_map/all_gather | solution.py:144
  566.2 30.4 all_gather.15
  607.4 35.0 all_to_all.45
  642.5 58.5 %collective-permute-done = bf16[640,2048]{1,0:T(8,128)(2,1)} collective-permute-done((bf16[640,2048]{1,0:T(8,128)(2,1)}, bf16[640,2048]{1,0:T(8,128)(2,1)}, u32[]{:S(2)}, u32[]{:S(2)}) %collective-permute-start) | collective-permute-done | bytes 2621472 | tf_op jit(solution)/shard_map/ppermute | solution.py:19
  708.1 113.8 %collective-permute-done.1 = bf16[1280,2048]{1,0:T(8,128)(2,1)} collective-permute-done((bf16[1280,2048]{1,0:T(8,128)(2,1)}, bf16[1280,2048]{1,0:T(8,128)(2,1)}, u32[]{:S(2)}, u32[]{:S(2)}) %collective-permute-start.1) | collective-permute-done | bytes 5242912 | tf_op jit(solution)/shard_map/ppermute | solution.py:19
  821.9 13.3 maximum_select_fusion.2
  835.2 450.8 %collective-permute-done.2 = bf16[2560,2048]{1,0:T(8,128)(2,1)} collective-permute-done((bf16[2560,2048]{1,0:T(8,128)(2,1)}, bf16[2560,2048]{1,0:T(8,128)(2,1)}, u32[]{:S(2)}, u32[]{:S(2)}) %collective-permute-start.2) | collective-permute-done | bytes 10485792 | tf_op jit(solution)/shard_map/ppermute | solution.py:19
  1286.1 27.4 fusion.44
  1313.4 33.1 multiply_convert_fusion.3
  1346.6 23.0 convolution_convert_fusion
  1369.6 341.8 %reduce-scatter.7.cloned.1.call-done = bf16[640,2048]{1,0:T(8,128)(2,1)} async-done(((bf16[5120,2048]{1,0:T(8,128)(2,1)}), bf16[640,2048]{1,0:T(8,128)(2,1)}) %reduce-scatter.7.cloned.1.call-update) | async-done | bytes 2621456 | tf_op jit(solution)/shard_map/reduce_scatter | solution.py:104
  1718.3 29.0 all-to-all-done.3
  1758.9 34.0 all_to_all.46
  1794.4 56.8 %collective-permute-done.3 = bf16[640,2048]{1,0:T(8,128)(2,1)S(1)} collective-permute-done((bf16[640,2048]{1,0:T(8,128)(2,1)S(1)}, bf16[640,2048]{1,0:T(8,128)(2,1)S(1)}, u32[]{:S(2)}, u32[]{:S(2)}) %collective-permute-start.3) | collective-permute-done | bytes 2621472 | tf_op jit(solution)/shard_map/ppermute | solution.py:19
  1859.1 113.4 %collective-permute-done.4 = bf16[1280,2048]{1,0:T(8,128)(2,1)S(1)} collective-permute-done((bf16[1280,2048]{1,0:T(8,128)(2,1)S(1)}, bf16[1280,2048]{1,0:T(8,128)(2,1)S(1)}, u32[]{:S(2)}, u32[]{:S(2)}) %collective-permute-start.4) | collective-permute-done | bytes 5242912 | tf_op jit(solution)/shard_map/ppermute | solution.py:19
  1972.5 18.2 maximum_select_fusion.3
  1996.3 448.9 %collective-permute-done.5 = bf16[2560,2048]{1,0:T(8,128)(2,1)S(1)} collective-permute-done((bf16[2560,2048]{1,0:T(8,128)(2,1)S(1)}, bf16[2560,2048]{1,0:T(8,128)(2,1)S(1)}, u32[]{:S(2)}, u32[]{:S(2)}) %collective-permute-start.5) | collective-permute-done | bytes 10485792 | tf_op jit(solution)/shard_map/ppermute | solution.py:19
  2449.1 35.2 multiply_convert_fusion.1
  2484.3 27.4 fusion.42
  2511.7 28.8 add_convert_fusion
  2540.5 343.0 %reduce-scatter.9.cloned.1.call-done = bf16[640,2048]{1,0:T(8,128)(2,1)} async-done(((bf16[5120,2048]{1,0:T(8,128)(2,1)}), bf16[640,2048]{1,0:T(8,128)(2,1)}) %reduce-scatter.9.cloned.1.call-update) | async-done | bytes 2621456 | tf_op jit(solution)/shard_map/reduce_scatter | solution.py:104
  2888.6 31.1 all-to-all-done.5
  2940.2 31.2 all-to-all-done.6
  2986.4 18.1 convert_bitcast_fusion
  3004.4 35.8 multiply_reduce_fusion
  3052.8 34.6 multiply_convert_fusion
  3087.4 12.5 fusion.14
  3128.2 90.5 %all-to-all-done.8 = bf16[4,256,4096]{1,2,0:T(8,128)(2,1)} async-done(((bf16[4,256,4096]{1,2,0:T(8,128)(2,1)}), bf16[4,256,4096]{1,2,0:T(8,128)(2,1)}, u32[]{:S(2)}, u32[]{:S(2)}) %all-to-all-start.8) | async-done | bytes 8388640 | tf_op jit(solution)/shard_map/all_to_all | solution.py:280
  3236.9 10.9 convolution_convert_fusion.2
  3255.1 11.8 multiply_convert_fusion.5
  3266.9 10.8 convolution_convert_fusion.3
  3277.8 24.3 convolution_bitcast_fusion
  3302.1 24.8 convolution_bitcast_fusion.1
  3348.1 24.3 convolution_bitcast_fusion.2
  3383.3 13.2 convolution_add_fusion.2
  3401.3 19.9 all-reduce.2
  3434.6 82.0 %reduce-scatter.11.cloned.1.call-done = bf16[256,4096]{1,0:T(8,128)(2,1)} async-done(((bf16[2048,4096]{1,0:T(8,128)(2,1)}), bf16[256,4096]{1,0:T(8,128)(2,1)}) %reduce-scatter.11.cloned.1.call-update) | async-done | bytes 2097168 | tf_op jit(solution)/shard_map/reduce_scatter | solution.py:305
  3516.6 152.1 %reduce-scatter.17.cloned.1.call-done = bf16[256,2048]{1,0:T(8,128)(2,1)} async-done(((bf16[2048,2048]{1,0:T(8,128)(2,1)}), bf16[256,2048]{1,0:T(8,128)(2,1)}) %reduce-scatter.17.cloned.1.call-update) | async-done | bytes 1048592 | tf_op jit(solution)/shard_map/reduce_scatter | solution.py:314
  3671.5 148.7 %reduce-scatter.15.cloned.1.call-done = bf16[256,2048]{1,0:T(8,128)(2,1)} async-done(((bf16[2048,2048]{1,0:T(8,128)(2,1)}), bf16[256,2048]{1,0:T(8,128)(2,1)}) %reduce-scatter.15.cloned.1.call-update) | async-done | bytes 1048592 | tf_op jit(solution)/shard_map/reduce_scatter | solution.py:311
  3823.1 50.1 %all-reduce.6.cloned.1.call-done = bf16[256,4096]{1,0:T(8,128)(2,1)} async-done(((bf16[256,4096]{1,0:T(8,128)(2,1)}), bf16[256,4096]{1,0:T(8,128)(2,1)}) %all-reduce.6.cloned.1.call-update) | async-done | bytes 2097168 | tf_op jit(solution)/shard_map/psum | solution.py:325
  (300 shorter events, 289.0 us)
Async XLA Ops:
  7.2 1339.4 %copy-start = (bf16[1,704,2048]{2,1,0:T(8,128)(2,1)S(1)}, bf16[1,704,2048]{2,1,0:T(8,128)(2,1)}, u32[]{:S(2)}) copy-start(bf16[1,704,2048]{2,1,0:T(8,128)(2,1)} %param.27) | copy-start | bytes 8650756
  7.2 233.3 %all-gather.7.cloned.1.call-start = ((), (), s32[]{:S(2)}) async-start(), calls=%async_computation.15 | async-start | bytes 18874368 | tf_op jit(solution)/shard_map/all_gather | solution.py:141
  7.9 357.8 %all-gather.11.cloned.1.call-start = ((), (), s32[]{:S(2)}) async-start(), calls=%async_computation.24 | async-start | bytes 9437184 | tf_op jit(solution)/shard_map/all_gather | solution.py:143
  8.7 415.7 %all-gather.9.cloned.1.call-start = ((), (), s32[]{:S(2)}) async-start(), calls=%async_computation.16 | async-start | bytes 10485760 | tf_op jit(solution)/shard_map/all_gather | solution.py:153
  10.2 253.2 %copy-start.54 = (f32[256]{0:T(256)}, f32[256]{0:T(256)S(1)}, u32[]{:S(2)}) copy-start(f32[256]{0:T(256)S(1)} %add_rsqrt_fusion.1) | copy-start | bytes 3076
  10.3 242.3 %copy-start.71 = (s32[1,1024,2]{1,2,0:T(2,128)S(1)}, s32[1,1024,2]{1,2,0:T(2,128)}, u32[]{:S(2)}) copy-start(s32[1,1024,2]{1,2,0:T(2,128)} %param.17) | copy-start | bytes 24580
  10.3 247.6 %copy-start.70 = (s32[1,1024,2]{1,2,0:T(2,128)S(1)}, s32[1,1024,2]{1,2,0:T(2,128)}, u32[]{:S(2)}) copy-start(s32[1,1024,2]{1,2,0:T(2,128)} %param.16) | copy-start | bytes 24580
  10.3 253.2 %copy-start.33 = (f32[2048]{0:T(1024)S(1)}, f32[2048]{0:T(1024)}, u32[]{:S(2)}) copy-start(f32[2048]{0:T(1024)} %param.19) | copy-start | bytes 24580
  263.4 342.2 %copy-start.25 = (s32[256,4]{0,1:T(4,128)}, s32[256,4]{0,1:T(4,128)S(1)}, u32[]{:S(2)}) copy-start(s32[256,4]{0,1:T(4,128)S(1)} %get-tuple-element.17) | copy-start | bytes 12292
  263.4 342.2 %copy-start.29 = (s32[256,4]{0,1:T(4,128)}, s32[256,4]{0,1:T(4,128)S(1)}, u32[]{:S(2)}) copy-start(s32[256,4]{0,1:T(4,128)S(1)} %get-tuple-element.18) | copy-start | bytes 12292
  267.2 36.0 all-to-all-start
  271.7 279.7 %all-gather.13.cloned.1.call-start = ((), (), s32[]{:S(2)}) async-start(), calls=%async_computation.25 | async-start | bytes 9437184 | tf_op jit(solution)/shard_map/all_gather | solution.py:144
  275.2 201.7 %copy-start.7 = (pred[640,1024]{1,0:T(8,128)(4,1)}, pred[640,1024]{1,0:T(8,128)(4,1)S(1)}, u32[]{:S(2)}) copy-start(pred[640,1024]{1,0:T(8,128)(4,1)S(1)} %fusion.48) | copy-start | bytes 1966084
  561.4 37.8 all-to-all-start.1
  566.1 1145.3 %reduce-scatter.7.cloned.1.call-start = ((), (), s32[]{:S(2)}) async-start(), calls=%async_computation.17 | async-start | bytes 23592960 | tf_op jit(solution)/shard_map/reduce_scatter | solution.py:104
  604.0 104.1 %copy-start.60 = (f32[256]{0:T(256)}, f32[256]{0:T(256)S(1)}, u32[]{:S(2)}) copy-start(f32[256]{0:T(256)S(1)} %add_rsqrt_fusion) | copy-start | bytes 3076
  642.4 58.6 %collective-permute-start = (bf16[640,2048]{1,0:T(8,128)(2,1)}, bf16[640,2048]{1,0:T(8,128)(2,1)}, u32[]{:S(2)}, u32[]{:S(2)}) collective-permute-start(bf16[640,2048]{1,0:T(8,128)(2,1)} %bitcast.30), channel_id=1, source_target_pairs={{0,4},{4,0},{8,12},{12,8},{16,20},{20,16},{24,28},{28,24},{1,5},{5... | collective-permute-start | bytes 7864328 | tf_op jit(solution)/shard_map/ppermute | solution.py:19
  708.1 113.8 %collective-permute-start.1 = (bf16[1280,2048]{1,0:T(8,128)(2,1)}, bf16[1280,2048]{1,0:T(8,128)(2,1)}, u32[]{:S(2)}, u32[]{:S(2)}) collective-permute-start(bf16[1280,2048]{1,0:T(8,128)(2,1)} %maximum_select_fusion.4), channel_id=1, source_target_pairs={{0,8},{4,12},{8,0},{12,4},{16,24},{20,28},{24,16},{28,20},{1,9},{5... | collective-permute-start | bytes 15728648 | tf_op jit(solution)/shard_map/ppermute | solution.py:19
  835.2 450.8 %collective-permute-start.2 = (bf16[2560,2048]{1,0:T(8,128)(2,1)}, bf16[2560,2048]{1,0:T(8,128)(2,1)}, u32[]{:S(2)}, u32[]{:S(2)}) collective-permute-start(bf16[2560,2048]{1,0:T(8,128)(2,1)} %maximum_select_fusion.2), channel_id=1, source_target_pairs={{0,16},{4,20},{8,24},{12,28},{16,0},{20,4},{24,8},{28,12},{1,17},{... | collective-permute-start | bytes 31457288 | tf_op jit(solution)/shard_map/ppermute | solution.py:19
  1369.5 347.2 %copy-start.18 = (bf16[2048,8]{0,1:T(8,128)(2,1)S(1)}, bf16[2048,8]{0,1:T(8,128)(2,1)}, u32[]{:S(2)}) copy-start(bf16[2048,8]{0,1:T(8,128)(2,1)} %copy-done.17) | copy-start | bytes 98308
  1369.5 377.8 %copy-start.26 = (s32[256,4]{0,1:T(4,128)S(1)}, s32[256,4]{0,1:T(4,128)}, u32[]{:S(2)}) copy-start(s32[256,4]{0,1:T(4,128)} %copy-done.25) | copy-start | bytes 12292
  1369.5 377.8 %copy-start.30 = (s32[256,4]{0,1:T(4,128)S(1)}, s32[256,4]{0,1:T(4,128)}, u32[]{:S(2)}) copy-start(s32[256,4]{0,1:T(4,128)} %copy-done.29) | copy-start | bytes 12292
  1711.4 35.9 all-to-all-start.3
  1716.0 1167.6 %reduce-scatter.9.cloned.1.call-start = ((), (), s32[]{:S(2)}) async-start(), calls=%async_computation.18 | async-start | bytes 23592960 | tf_op jit(solution)/shard_map/reduce_scatter | solution.py:104
  1792.9 58.2 %collective-permute-start.3 = (bf16[640,2048]{1,0:T(8,128)(2,1)S(1)}, bf16[640,2048]{1,0:T(8,128)(2,1)S(1)}, u32[]{:S(2)}, u32[]{:S(2)}) collective-permute-start(bf16[640,2048]{1,0:T(8,128)(2,1)S(1)} %bitcast.241), channel_id=1, source_target_pairs={{0,4},{4,0},{8,12},{12,8},{16,20},{20,16},{24,28},{28,24},{1,5},{5... | collective-permute-start | bytes 7864328 | tf_op jit(solution)/shard_map/ppermute | solution.py:19
  1858.9 113.6 %collective-permute-start.4 = (bf16[1280,2048]{1,0:T(8,128)(2,1)S(1)}, bf16[1280,2048]{1,0:T(8,128)(2,1)S(1)}, u32[]{:S(2)}, u32[]{:S(2)}) collective-permute-start(bf16[1280,2048]{1,0:T(8,128)(2,1)S(1)} %maximum_select_fusion.5), channel_id=1, source_target_pairs={{0,8},{4,12},{8,0},{12,4},{16,24},{20,28},{24,16},{28,20},{1,9},{5... | collective-permute-start | bytes 15728648 | tf_op jit(solution)/shard_map/ppermute | solution.py:19
  1994.7 450.5 %collective-permute-start.5 = (bf16[2560,2048]{1,0:T(8,128)(2,1)S(1)}, bf16[2560,2048]{1,0:T(8,128)(2,1)S(1)}, u32[]{:S(2)}, u32[]{:S(2)}) collective-permute-start(bf16[2560,2048]{1,0:T(8,128)(2,1)S(1)} %maximum_select_fusion.3), channel_id=1, source_target_pairs={{0,16},{4,20},{8,24},{12,28},{16,0},{20,4},{24,8},{28,12},{1,17},{... | collective-permute-start | bytes 31457288 | tf_op jit(solution)/shard_map/ppermute | solution.py:19
  2540.4 347.9 %copy-start.45 = (s32[256,4]{0,1:T(4,128)S(1)}, s32[256,4]{0,1:T(4,128)}, u32[]{:S(2)}) copy-start(s32[256,4]{0,1:T(4,128)} %copy-done.43) | copy-start | bytes 12292
  2540.4 347.9 %copy-start.49 = (s32[256,4]{0,1:T(4,128)S(1)}, s32[256,4]{0,1:T(4,128)}, u32[]{:S(2)}) copy-start(s32[256,4]{0,1:T(4,128)} %copy-done.47) | copy-start | bytes 12292
  2540.4 347.9 %copy-start.68 = (f32[256,4]{0,1:T(4,128)S(1)}, f32[256,4]{0,1:T(4,128)}, u32[]{:S(2)}) copy-start(f32[256,4]{0,1:T(4,128)} %copy-done.67) | copy-start | bytes 12292
  2540.4 379.2 %copy-start.27 = (s32[256,4]{0,1:T(4,128)S(1)}, s32[256,4]{0,1:T(4,128)}, u32[]{:S(2)}) copy-start(s32[256,4]{0,1:T(4,128)} %copy-done.25) | copy-start | bytes 12292
  2540.5 379.2 %copy-start.31 = (s32[256,4]{0,1:T(4,128)S(1)}, s32[256,4]{0,1:T(4,128)}, u32[]{:S(2)}) copy-start(s32[256,4]{0,1:T(4,128)} %copy-done.29) | copy-start | bytes 12292
  2540.5 383.6 %copy-start.4 = (f32[256,2048]{1,0:T(8,128)S(1)}, f32[256,2048]{1,0:T(8,128)}, u32[]{:S(2)}) copy-start(f32[256,2048]{1,0:T(8,128)} %copy-done.3) | copy-start | bytes 6291460
  2540.5 383.6 %copy-start.19 = (bf16[2048,8]{0,1:T(8,128)(2,1)S(1)}, bf16[2048,8]{0,1:T(8,128)(2,1)}, u32[]{:S(2)}) copy-start(bf16[2048,8]{0,1:T(8,128)(2,1)} %copy-done.17) | copy-start | bytes 98308
  2540.5 383.6 %copy-start.37 = (f32[2048]{0:T(1024)S(1)}, f32[2048]{0:T(1024)}, u32[]{:S(2)}) copy-start(f32[2048]{0:T(1024)} %param.20) | copy-start | bytes 24580
  2540.5 383.6 %copy-start.53 = (f32[256,4]{0,1:T(4,128)S(1)}, f32[256,4]{0,1:T(4,128)}, u32[]{:S(2)}) copy-start(f32[256,4]{0,1:T(4,128)} %get-tuple-element.20) | copy-start | bytes 12292
  2540.5 383.6 %copy-start.61 = (f32[256]{0:T(256)S(1)}, f32[256]{0:T(256)}, u32[]{:S(2)}) copy-start(f32[256]{0:T(256)} %copy-done.60) | copy-start | bytes 3076
  2883.6 36.1 all-to-all-start.5
  2936.3 35.2 all-to-all-start.6
  3119.8 99.0 %all-to-all-start.8 = ((bf16[4,256,4096]{1,2,0:T(8,128)(2,1)}), bf16[4,256,4096]{1,2,0:T(8,128)(2,1)}, u32[]{:S(2)}, u32[]{:S(2)}) async-start(bf16[4,256,4096]{1,2,0:T(8,128)(2,1)} %pad_maximum_fusion), calls=%async_computation.10 | async-start | bytes 16777216 | tf_op jit(solution)/shard_map/all_to_all | solution.py:280
  3125.6 295.8 %reduce-scatter.13.cloned.1.call-start = ((), (), s32[]{:S(2)}) async-start(), calls=%async_computation.21 | async-start | bytes 36864 | tf_op jit(solution)/shard_map/reduce_scatter | solution.py:308
  3126.8 108.4 %copy-start.63 = (f32[256,4]{0,1:T(4,128)}, f32[256,4]{0,1:T(4,128)S(1)}, u32[]{:S(2)}) copy-start(f32[256,4]{0,1:T(4,128)S(1)} %select_reduce_fusion.1) | copy-start | bytes 12292
  3128.2 388.4 %reduce-scatter.11.cloned.1.call-start = ((), (), s32[]{:S(2)}) async-start(), calls=%async_computation.19 | async-start | bytes 18874368 | tf_op jit(solution)/shard_map/reduce_scatter | solution.py:305
  3235.2 433.5 %reduce-scatter.17.cloned.1.call-start = ((), (), s32[]{:S(2)}) async-start(), calls=%async_computation.23 | async-start | bytes 9437184 | tf_op jit(solution)/shard_map/reduce_scatter | solution.py:314
  3247.9 572.4 %reduce-scatter.15.cloned.1.call-start = ((), (), s32[]{:S(2)}) async-start(), calls=%async_computation.22 | async-start | bytes 9437184 | tf_op jit(solution)/shard_map/reduce_scatter | solution.py:311
  3344.3 34.9 all-to-all-start.7
  3348.0 525.1 %all-reduce.6.cloned.1.call-start = ((), (), s32[]{:S(2)}) async-start(), calls=%async_computation.20 | async-start | bytes 4194304 | tf_op jit(solution)/shard_map/psum | solution.py:325
  3516.6 360.7 %copy-start.1 = (bf16[1,704,2048]{2,1,0:T(8,128)(2,1)S(1)}, bf16[1,704,2048]{2,1,0:T(8,128)(2,1)}, u32[]{:S(2)}) copy-start(bf16[1,704,2048]{2,1,0:T(8,128)(2,1)} %param.27) | copy-start | bytes 8650756
  (54 other events, 943.5 us)
Sparse Core Ops, SparseCore 0:
  10.2 230.2 all-gather.6
  242.6 123.1 all-gather.10
  367.9 56.4 all-gather.8
  426.4 124.9 all-gather.12
  1369.7 341.6 reduce-scatter.6
  2540.6 342.9 reduce-scatter.8
  3129.6 53.1 reduce-scatter.12
  3235.4 281.1 reduce-scatter.10
  3520.7 148.0 reduce-scatter.16
  3672.2 147.9 reduce-scatter.14
  3822.8 50.3 all-reduce.5
